TPU v7x, 256 devices: a whole 4x4x8 slice. The times are simulated.
256 devices in a mesh: wide: 64 (over y, z, core), narrow: 4 (over x).
Axes of the slice: x: 4, y: 4, z: 8, core: 2. Of those that a mesh axis runs over, the one named last changes fastest.
Arguments:
- diag_block: float32 [256, 512, 512], P('wide', None, 'narrow'), as said below
- panel: float32 [256, 1024, 512], P('wide', None, 'narrow'), may hold values from -2 to 2
- panel_count: int32 [256], P('wide'), may hold values from 1 to 8, 1152 in all
- pair_owner: int32 [9216, 1], P('wide'), may hold values from 0 to 63; in each aligned block of 144 rows (0 to 143, 144 to 287, ...) at most 3 rows name the same one
- pair_slot: int32 [9216], P('wide'), may hold values from 0 to 7
- ancestor: float32 [512, 128, 128], P(('wide', 'narrow')), may hold values from -6 to 6
Outputs:
- factor: float32 [256, 512, 512], P('wide', None, 'narrow')
- lower_panel: float32 [256, 1024, 512], P('wide', None, 'narrow')
- updated: float32 [512, 128, 128], P(('wide', 'narrow'))
Inputs may be any that keep to these rules, and one draw needn't show every extreme that they name: Each diag_block[s] is symmetric, and its least eigenvalue is 0.2 or more. `pair_owner`: among the rows of one index of wide no owner is named more than 3 times, a bound that some block reaches.
All inputs are finite; a program needn't handle non-finite values. No bound on the sum of `panel_count` on one device may be relied on, other than what follows from the above.
Results may differ from a plain program's by a relative error of at most 0.00016.
Values sent between devices are 32-bit elements; how exact they have to be, the bound alone decides.
A program may use at most 128 MiB of HBM per device.

v0:
```python
import jax
import jax.numpy as jnp
import numpy as np
from jax import lax
from jax.sharding import PartitionSpec as P

W = 512
B = 128
P_SIZE = 8
T_DEV = 2


def pair_lists(count):
    first = []
    second = []
    for outer in range(count):
        for inner in range(outer + 1):
            first.append(outer)
            second.append(inner)
    return (np.array(first, np.int32), np.array(second, np.int32))


def local(diag_block, panel, panel_count, pair_owner, pair_slot, ancestor):
    supers_here = diag_block.shape[0]
    col_width = diag_block.shape[2]
    narrow_index = lax.axis_index("narrow")
    narrow_count = lax.axis_size("narrow")
    wide_count = lax.axis_size("wide")
    col_start = narrow_index * col_width
    whole_diag = lax.all_gather(diag_block, "narrow", axis=2, tiled=True)
    factor = jnp.linalg.cholesky(whole_diag)
    identity = jnp.broadcast_to(jnp.eye(W, dtype=jnp.float32), factor.shape)
    inverse = lax.linalg.triangular_solve(factor, identity, left_side=True, lower=True)
    inverse_t = jnp.swapaxes(inverse, 1, 2)
    own_cols = lax.dynamic_slice_in_dim(inverse_t, col_start, col_width, 2)
    lower_panel = jnp.einsum(
        "srk,skc->src",
        lax.all_gather(panel, "narrow", axis=2, tiled=True),
        own_cols,
        precision=lax.Precision.HIGHEST,
    )
    block_index = jnp.arange(P_SIZE * B, dtype=jnp.int32) // B
    live = (block_index[None, :] < panel_count[:, None]).astype(jnp.float32)
    lower_panel = lower_panel * live[:, :, None]
    first, second = pair_lists(P_SIZE)
    blocks = lower_panel.reshape(supers_here, P_SIZE, B, col_width)
    partial_updates = jnp.einsum(
        "spac,spbc->spab", blocks[:, first], blocks[:, second], precision=lax.Precision.HIGHEST
    )
    pair_rows = supers_here * len(first)
    partial_updates = partial_updates.reshape(pair_rows, B, B)
    capacity = max(2, (pair_rows + wide_count - 1) // wide_count)
    owners = pair_owner[:, 0]
    owner_table = (owners[:, None] == jnp.arange(wide_count, dtype=jnp.int32)[None, :]).astype(
        jnp.int32
    )
    earlier = jnp.cumsum(owner_table, axis=0) - owner_table
    rank_here = jnp.sum(earlier * owner_table, axis=1)
    position = owners * capacity + rank_here
    buffer_rows = wide_count * capacity
    row_slots = T_DEV * narrow_count
    slot_ids = jnp.full((buffer_rows,), -1, jnp.int32).at[position].set(pair_slot)
    send_buffer = jnp.zeros((buffer_rows, B, B), jnp.float32).at[position].set(partial_updates)
    received, got_slots = (
        lax.all_to_all(send_buffer, "wide", split_axis=0, concat_axis=0, tiled=True),
        lax.all_to_all(slot_ids, "wide", split_axis=0, concat_axis=0, tiled=True),
    )
    slot_table = (got_slots[:, None] == jnp.arange(row_slots, dtype=jnp.int32)[None, :]).astype(
        jnp.float32
    )
    row_sums = jnp.einsum("ri,rab->iab", slot_table, received, precision=lax.Precision.HIGHEST)
    summed = lax.psum_scatter(row_sums, "narrow", scatter_dimension=0, tiled=True)
    factor_cols = lax.dynamic_slice_in_dim(factor, col_start, col_width, 2)
    return (factor_cols, lower_panel, ancestor - summed)


def solution(mesh):
    placed = (
        P("wide", None, "narrow"),
        P("wide", None, "narrow"),
        P("wide"),
        P("wide", None),
        P("wide"),
        P(("wide", "narrow"), None, None),
    )
    return jax.shard_map(
        local,
        mesh=mesh,
        in_specs=placed,
        out_specs=(
            P("wide", None, "narrow"),
            P("wide", None, "narrow"),
            P(("wide", "narrow"), None, None),
        ),
        check_vma=False,
    )
```

profile of v0, /device:TPU:8, one launch (start us, length us, event | category | flops | bytes accessed | tf_op | source)
XLA Modules:
  0.0 1013.3 jit_solution(1670821156970173186)
XLA Ops:
  7.3 2.5 copy.74
  9.9 0.7 all-gather.5.cloned.1.call-update
  10.6 0.6 reduce-window.6
  11.2 0.2 slice_reduce_fusion
  11.6 1.2 scatter_custom_fusion
  12.8 0.8 all_to_all.9
  13.6 12.4 %all-to-all-start = ((s32[64,3,1]{1,2,0:T(1,128)}), s32[64,3,1]{1,2,0:T(1,128)S(1)}, u32[]{:S(2)}, u32[]{:S(2)}) async-start(s32[64,3,1]{1,2,0:T(1,128)} %bitcast.20), calls=%async_computation | async-start | bytes 65536 | tf_op jit(solution)/shard_map/all_to_all | solution.py:66
  26.4 0.8 fusion.61
  27.2 36.9 %all-gather.3.cloned.1.call-done = f32[4,512,512]{1,2,0:T(8,128)} async-done(((f32[4,512,128]{1,2,0:T(8,128)}), f32[4,512,512]{1,2,0:T(8,128)}) %all-gather.3.cloned.1.call-update) | async-done | bytes 4194320 | tf_op jit(solution)/shard_map/all_gather | solution.py:30
  64.1 5.3 copy.75
  69.4 4.5 fusion.5
  73.9 2.0 copy-done.1
  75.9 46.9 %custom-call.34 = f32[4,128,128]{2,1,0:T(8,128)S(1)} custom-call(f32[4,128,128]{2,1,0:T(8,128)S(1)} %cholesky.274), custom_call_target="Cholesky" | custom-call | tf_op jit(solution)/shard_map/jit(cholesky)/cholesky | solution.py:31
  122.8 39.3 %custom-call.35 = f32[4,1,128,128]{2,3,1,0:T(8,128)S(1)} custom-call(f32[4,1,128,128]{3,2,1,0:T(8,128)S(1)} %select_bitcast_fusion.2), custom_call_target="InvertDiagBlocksLowerTriangular" | custom-call | tf_op jit(solution)/shard_map/jit(cholesky)/cholesky | solution.py:31
  162.2 2.5 cholesky.234
  164.7 3.0 constant_dynamic-update-slice_fusion.3
  167.6 2.0 convolution_subtract_fusion.1
  169.6 47.1 %custom-call.36 = f32[4,128,128]{2,1,0:T(8,128)S(1)} custom-call(f32[4,128,128]{2,1,0:T(8,128)S(1)} %cholesky.278), custom_call_target="Cholesky" | custom-call | tf_op jit(solution)/shard_map/jit(cholesky)/cholesky | solution.py:31
  216.8 0.8 select_bitcast_fusion.1
  217.6 39.3 %custom-call.37 = f32[4,1,128,128]{2,3,1,0:T(8,128)S(1)} custom-call(f32[4,1,128,128]{3,2,1,0:T(8,128)S(1)} %get-tuple-element.46), custom_call_target="InvertDiagBlocksLowerTriangular" | custom-call | tf_op jit(solution)/shard_map/jit(cholesky)/cholesky | solution.py:31
  256.9 1.4 convolution_dynamic-update-slice_fusion
  258.3 2.6 convolution_subtract_fusion.2
  260.9 46.9 %custom-call.38 = f32[4,128,128]{2,1,0:T(8,128)S(1)} custom-call(f32[4,128,128]{2,1,0:T(8,128)S(1)} %cholesky.283), custom_call_target="Cholesky" | custom-call | tf_op jit(solution)/shard_map/jit(cholesky)/cholesky | solution.py:31
  307.8 0.8 select_bitcast_fusion
  308.6 39.8 %custom-call.39 = f32[4,1,128,128]{2,3,1,0:T(8,128)S(1)} custom-call(f32[4,1,128,128]{3,2,1,0:T(8,128)S(1)} %get-tuple-element.44), custom_call_target="InvertDiagBlocksLowerTriangular" | custom-call | tf_op jit(solution)/shard_map/jit(cholesky)/cholesky | solution.py:31
  348.4 1.1 convolution_dynamic-update-slice_fusion.1
  349.5 2.6 convolution_subtract_fusion.3
  352.1 46.9 %custom-call.40 = f32[4,128,128]{2,1,0:T(8,128)S(1)} custom-call(f32[4,128,128]{2,1,0:T(8,128)S(1)} %convolution_subtract_fusion.3), custom_call_target="Cholesky" | custom-call | tf_op jit(solution)/shard_map/jit(cholesky)/cholesky | solution.py:31
  399.0 0.8 select_reduce_fusion.2
  400.0 0.2 compare_reduce_fusion
  400.2 6.7 broadcast_select_fusion
  406.9 15.0 %while.1 = (s32[]{:T(128)}, f32[4,512,512]{2,1,0:T(8,128)}, s32[4,2]{0,1:T(2,128)S(1)}, f32[4,4,128,128]{3,2,0,1:T(8,128)}, s32[]{:T(128)}) while((s32[]{:T(128)}, f32[4,512,512]{2,1,0:T(8,128)}, s32[4,2]{0,1:T(2,128)S(1)}, f32[4,4,128,128]{3,2,0,1:T(8,128)}, s32[]{:T(128)}) %tuple.40), condition=%wide.while_cond, body=%wide.while_body.sunk | while | flops 2 | bytes 525421 | solution.py:33
  407.0 0.5 fusion.71
  407.5 3.2 bitcast_dynamic-update-slice_fusion.2
  410.8 0.5 fusion.71
  411.3 3.2 bitcast_dynamic-update-slice_fusion.2
  414.6 0.5 fusion.71
  415.1 3.2 bitcast_dynamic-update-slice_fusion.2
  418.3 0.5 fusion.71
  418.9 3.1 bitcast_dynamic-update-slice_fusion.2
  421.9 158.2 %custom-call.41 = f32[4,4,128,128]{2,3,1,0:T(8,128)S(1)} custom-call(f32[4,4,128,128]{3,2,1,0:T(8,128)} %bitcast.100), custom_call_target="InvertDiagBlocksLowerTriangular" | custom-call | tf_op jit(solution)/shard_map/triangular_solve | solution.py:33
  580.1 1.0 fusion.35
  581.2 2.0 convolution_subtract_fusion
  583.1 1.1 fusion.40
  584.2 2.4 fusion.19
  586.7 2.0 fusion.38
  588.7 3.3 fusion.16
  592.0 3.1 fusion.37
  595.1 13.3 %multiply_bitcast_fusion = f32[4,1024,128]{1,2,0:T(8,128)} fusion(f32[4,1024,512]{2,1,0:T(8,128)} %all-gather.5.cloned.1.call-done, s32[]{:T(128)S(6)} %select_n.29, f32[4,128,512]{2,1,0:T(8,128)S(1)} %fusion.35, f32[4,128,512]{2,1,0:T(8,128)S(1)} %fusion.40, f32[4,128,512]{2,1,0:T(8,128)S(1)} %fusion.38, f32[4,128,512]{2,1,0:T(8,128)} %fusion.37, ...), kind=kOutput, calls=%fused_computation.28 | convolution fusion | flops 3222536192 | bytes 14696452 | tf_op jit(solution)/shard_map/srk,skc->src/dot_general | solution.py:36
  608.4 1.9 copy.96
  610.3 6.7 gather_fusion.1
  617.1 6.7 gather_fusion
  623.8 25.8 %fusion.2 = f32[4,36,128,128]{3,2,1,0:T(8,128)} fusion(f32[36,4,128,128]{3,2,1,0:T(8,128)} %gather_fusion.1, f32[36,4,128,128]{3,2,1,0:T(8,128)} %gather_fusion), kind=kOutput, calls=%fused_computation.8 | convolution fusion | flops 3623878656 | bytes 28311552 | tf_op jit(solution)/shard_map/spac,spbc->spab/dot_general | solution.py:47
  649.6 6.2 broadcast_in_dim.43
  655.7 26.3 %scatter_fusion = f32[192,128,128]{2,1,0:T(8,128)} fusion(f32[192,128,128]{2,1,0:T(8,128)} %broadcast_in_dim.43, s32[144]{0:T(256)S(1)} %bitcast.98, f32[144,128,128]{2,1,0:T(8,128)} %bitcast.94), kind=kCustom, calls=%fused_computation.3 | custom fusion | bytes 28312128 | tf_op jit(solution)/shard_map/scatter | solution.py:63
  682.1 10.7 %all-to-all-start.1 = ((f32[192,128,128]{2,1,0:T(8,128)}), f32[192,128,128]{2,1,0:T(8,128)}, u32[]{:S(2)}, u32[]{:S(2)}) async-start(f32[192,128,128]{2,1,0:T(8,128)} %scatter_fusion), calls=%async_computation.1 | async-start | bytes 25165824 | tf_op jit(solution)/shard_map/all_to_all | solution.py:65
  692.9 0.5 broadcast.291
  693.4 0.7 reduce.29
  694.2 273.1 %all-to-all-done.1 = f32[192,128,128]{2,1,0:T(8,128)} async-done(((f32[192,128,128]{2,1,0:T(8,128)}), f32[192,128,128]{2,1,0:T(8,128)}, u32[]{:S(2)}, u32[]{:S(2)}) %all-to-all-start.1) | async-done | bytes 12582944 | tf_op jit(solution)/shard_map/all_to_all | solution.py:65
  967.4 15.5 %fusion = f32[8,128,128]{2,0,1:T(8,128)S(1)} fusion(f32[192,128,128]{2,1,0:T(8,128)} %all-to-all-done.1, s32[192]{0:T(256)S(1)} %eq.54), kind=kOutput, calls=%fused_computation.6 | convolution fusion | flops 301991424 | bytes 13107968 | tf_op jit(solution)/shard_map/ri,rab->iab/dot_general | solution.py:71
  982.8 0.9 copy.95
  983.7 2.3 constant_dynamic-slice_fusion.1
  986.0 18.7 %reduce-scatter.2.cloned.1.call-done = f32[2,128,128]{2,1,0:T(8,128)} async-done(((f32[8,128,128]{2,1,0:T(8,128)}), f32[2,128,128]{2,1,0:T(8,128)}) %reduce-scatter.2.cloned.1.call-update) | async-done | bytes 131088 | tf_op jit(solution)/shard_map/reduce_scatter | solution.py:72
  1004.7 1.6 sub.14
  (51 shorter events, 1.4 us)
Async XLA Ops:
  7.2 18.9 %copy-start.6 = (s32[36]{0:T(128)S(1)}, s32[36]{0:T(128)}, u32[]{:S(2)}) copy-start(s32[36]{0:T(128)} %constant.237) | copy-start | bytes 436
  7.2 18.9 %copy-start.5 = (s32[36]{0:T(128)S(1)}, s32[36]{0:T(128)}, u32[]{:S(2)}) copy-start(s32[36]{0:T(128)} %constant.238) | copy-start | bytes 436
  7.2 3.4 copy-start.4
  7.2 19.1 %copy-start.7 = (s32[4]{0:T(128)S(1)}, s32[4]{0:T(128)}, u32[]{:S(2)}) copy-start(s32[4]{0:T(128)} %param.12) | copy-start | bytes 52
  7.2 56.9 %all-gather.3.cloned.1.call-start = ((), (), s32[]{:S(2)}) async-start(), calls=%async_computation.3 | async-start | bytes 5242880 | tf_op jit(solution)/shard_map/all_gather | solution.py:30
  9.8 585.3 %all-gather.5.cloned.1.call-start = ((), (), s32[]{:S(2)}) async-start(), calls=%async_computation.4 | async-start | bytes 10485760 | tf_op jit(solution)/shard_map/all_gather | solution.py:38
  13.6 668.5 %all-to-all-start = ((s32[64,3,1]{1,2,0:T(1,128)}), s32[64,3,1]{1,2,0:T(1,128)S(1)}, u32[]{:S(2)}, u32[]{:S(2)}) async-start(s32[64,3,1]{1,2,0:T(1,128)} %bitcast.20), calls=%async_computation | async-start | bytes 65536 | tf_op jit(solution)/shard_map/all_to_all | solution.py:66
  73.9 2.0 copy-start.1
  580.1 4.1 copy-start.2
  610.3 6.8 copy-start
  682.1 285.3 %all-to-all-start.1 = ((f32[192,128,128]{2,1,0:T(8,128)}), f32[192,128,128]{2,1,0:T(8,128)}, u32[]{:S(2)}, u32[]{:S(2)}) async-start(f32[192,128,128]{2,1,0:T(8,128)} %scatter_fusion), calls=%async_computation.1 | async-start | bytes 25165824 | tf_op jit(solution)/shard_map/all_to_all | solution.py:65
  692.8 311.9 %reduce-scatter.2.cloned.1.call-start = ((), (), s32[]{:S(2)}) async-start(), calls=%async_computation.5 | async-start | bytes 655360 | tf_op jit(solution)/shard_map/reduce_scatter | solution.py:72
  694.2 310.5 %copy-start.3 = (f32[2,128,128]{2,1,0:T(8,128)S(1)}, f32[2,128,128]{2,1,0:T(8,128)}, u32[]{:S(2)}) copy-start(f32[2,128,128]{2,1,0:T(8,128)} %param.15) | copy-start | bytes 393220
Sparse Core Ops, SparseCore 0:
  10.4 53.6 all-gather.2
  65.9 90.4 all-gather.4
  983.9 20.7 reduce-scatter.1
where the time goes:
time: 1020 us; the launch traced here: 1010 us
  other arithmetic  482 us (47%)
  waiting for transfers between devices  329 us (32%)
  matrix products  82.2 us (8%)
  local copies, waits for them, and re-layouts  82 us (8%)
  starting transfers between devices  23.3 us (2%)
  between operations  14.6 us (1%)
    another operation x16, other arithmetic, local(): factor = jnp.linalg.cholesky(whole_diag)  309 us
    all_to_all x1, waiting for transfers between devices, local(): lax.all_to_all(send_buffer, 'wide', split_axis=0, concat_axis=0, tiled=True)  273 us
    another operation x3, other arithmetic, local(): lax.linalg.triangular_solve(factor, identity, left_side=True, lower=True)  165 us
    all_gather x1, waiting for transfers between devices, local(): whole_diag = lax.all_gather(diag_block, 'narrow', axis=2, tiled=True)  36.9 us
    scatter x1, local copies, waits for them, and re-layouts, local(): jnp.zeros((buffer_rows, B, B), jnp.float32).at[position]  26.3 us
    dot_general x1, matrix products, local(): jnp.einsum('spac,spbc->spab', blocks[:, first], blocks[:, second], precis...  25.8 us
  transfers between devices with their start and end apart: 5, of which 3 were waited for; matrix products, arithmetic and copies ran while one was open for 61% of the time, Pallas kernels for 0%

commit v1 on v0

--- a/solution.py
+++ b/solution.py
@@ -3,6 +3,7 @@
 import numpy as np
 from jax import lax
 from jax.sharding import PartitionSpec as P
+from jax.lax import all_to_all, axis_size
 
 W = 512
 B = 128
@@ -27,7 +28,9 @@
     narrow_count = lax.axis_size("narrow")
     wide_count = lax.axis_size("wide")
     col_start = narrow_index * col_width
-    whole_diag = lax.all_gather(diag_block, "narrow", axis=2, tiled=True)
+    whole_diag = jnp.concatenate(
+        all_to_all(jnp.stack([diag_block] * axis_size("narrow")), "narrow", 0, 0), 2
+    )
     factor = jnp.linalg.cholesky(whole_diag)
     identity = jnp.broadcast_to(jnp.eye(W, dtype=jnp.float32), factor.shape)
     inverse = lax.linalg.triangular_solve(factor, identity, left_side=True, lower=True)

time: 1020 us -> 1070 us (1.049)
  waiting for transfers between devices: 329 us -> 370 us
    all_to_all x0 -> x1, waiting for transfers between devices: none -> 74.9 us  [local(): all_to_all(jnp.stack([diag_block] * axis_size('narrow')), 'narrow', 0, 0)]
    all_gather x1 -> x0, waiting for transfers between devices: 36.9 us -> none  [local(): whole_diag = lax.all_gather(diag_block, 'narrow', axis=2, tiled=True)]
  transfers between devices with their start and end apart: 5 -> 5, of which waited for: 3 -> 3; matrix products, arithmetic and copies ran while one was open for 61% -> 59% of each run, Pallas kernels for 0% -> 0%
where the time goes in v1:
time: 1070 us
  other arithmetic  482 us (45%)
  waiting for transfers between devices  370 us (35%)
  local copies, waits for them, and re-layouts  88.5 us (8%)
  matrix products  82.2 us (8%)
  starting transfers between devices  29.7 us (3%)
  between operations  14.8 us (1%)
    another operation x16, other arithmetic, local(): factor = jnp.linalg.cholesky(whole_diag)  309 us
    all_to_all x1, waiting for transfers between devices, local(): lax.all_to_all(send_buffer, 'wide', split_axis=0, concat_axis=0, tiled=True)  273 us
    another operation x3, other arithmetic, local(): lax.linalg.triangular_solve(factor, identity, left_side=True, lower=True)  165 us
    all_to_all x1, waiting for transfers between devices, local(): all_to_all(jnp.stack([diag_block] * axis_size('narrow')), 'narrow', 0, 0)  74.9 us
    scatter x1, local copies, waits for them, and re-layouts, local(): jnp.zeros((buffer_rows, B, B), jnp.float32).at[position]  26.3 us
    dot_general x1, matrix products, local(): jnp.einsum('spac,spbc->spab', blocks[:, first], blocks[:, second], precis...  25.8 us
  transfers between devices with their start and end apart: 5, of which 3 were waited for; matrix products, arithmetic and copies ran while one was open for 59% of the time, Pallas kernels for 0%

profile of v1, /device:TPU:8, one launch (start us, length us, event | category | flops | bytes accessed | tf_op | source)
XLA Modules:
  0.0 1067.0 jit_solution(18202277091695760639)
XLA Ops:
  7.2 0.7 all-gather.2.cloned.1.call-update
  7.9 1.6 copy.75
  9.5 2.5 stack.2
  12.0 5.1 all-to-all-start
  17.1 0.6 reduce-window.6
  18.1 1.2 scatter_custom_fusion
  19.3 0.8 all_to_all.13
  20.5 0.8 fusion.61
  21.3 74.9 %all-to-all-done = f32[4,4,512,128]{2,3,1,0:T(8,128)} async-done(((f32[4,4,512,128]{2,3,1,0:T(8,128)}), f32[4,4,512,128]{2,3,1,0:T(8,128)}, u32[]{:S(2)}, u32[]{:S(2)}) %all-to-all-start) | async-done | bytes 4194336 | tf_op jit(solution)/shard_map/all_to_all | solution.py:32
  96.2 14.0 %all-to-all-start.1 = ((s32[64,3,1]{1,2,0:T(1,128)}), s32[64,3,1]{1,2,0:T(1,128)S(1)}, u32[]{:S(2)}, u32[]{:S(2)}) async-start(s32[64,3,1]{1,2,0:T(1,128)} %bitcast.22), calls=%async_computation.1 | async-start | bytes 65536 | tf_op jit(solution)/shard_map/all_to_all | solution.py:69
  110.2 4.8 copy.76
  114.9 5.3 copy.77
  120.2 4.6 fusion.5
  124.9 2.0 copy-done.1
  126.9 46.9 %custom-call.34 = f32[4,128,128]{2,1,0:T(8,128)S(1)} custom-call(f32[4,128,128]{2,1,0:T(8,128)S(1)} %cholesky.274), custom_call_target="Cholesky" | custom-call | tf_op jit(solution)/shard_map/jit(cholesky)/cholesky | solution.py:34
  173.8 39.3 %custom-call.35 = f32[4,1,128,128]{2,3,1,0:T(8,128)S(1)} custom-call(f32[4,1,128,128]{3,2,1,0:T(8,128)S(1)} %select_bitcast_fusion.2), custom_call_target="InvertDiagBlocksLowerTriangular" | custom-call | tf_op jit(solution)/shard_map/jit(cholesky)/cholesky | solution.py:34
  213.1 2.5 cholesky.234
  215.6 3.0 constant_dynamic-update-slice_fusion.3
  218.6 2.0 convolution_subtract_fusion.1
  220.6 47.1 %custom-call.36 = f32[4,128,128]{2,1,0:T(8,128)S(1)} custom-call(f32[4,128,128]{2,1,0:T(8,128)S(1)} %cholesky.278), custom_call_target="Cholesky" | custom-call | tf_op jit(solution)/shard_map/jit(cholesky)/cholesky | solution.py:34
  267.7 0.8 select_bitcast_fusion.1
  268.5 39.3 %custom-call.37 = f32[4,1,128,128]{2,3,1,0:T(8,128)S(1)} custom-call(f32[4,1,128,128]{3,2,1,0:T(8,128)S(1)} %get-tuple-element.46), custom_call_target="InvertDiagBlocksLowerTriangular" | custom-call | tf_op jit(solution)/shard_map/jit(cholesky)/cholesky | solution.py:34
  307.8 1.4 convolution_dynamic-update-slice_fusion
  309.3 2.6 convolution_subtract_fusion.2
  311.9 46.9 %custom-call.38 = f32[4,128,128]{2,1,0:T(8,128)S(1)} custom-call(f32[4,128,128]{2,1,0:T(8,128)S(1)} %cholesky.283), custom_call_target="Cholesky" | custom-call | tf_op jit(solution)/shard_map/jit(cholesky)/cholesky | solution.py:34
  358.8 0.8 select_bitcast_fusion
  359.5 39.8 %custom-call.39 = f32[4,1,128,128]{2,3,1,0:T(8,128)S(1)} custom-call(f32[4,1,128,128]{3,2,1,0:T(8,128)S(1)} %get-tuple-element.44), custom_call_target="InvertDiagBlocksLowerTriangular" | custom-call | tf_op jit(solution)/shard_map/jit(cholesky)/cholesky | solution.py:34
  399.3 1.1 convolution_dynamic-update-slice_fusion.1
  400.4 2.6 convolution_subtract_fusion.3
  403.1 46.9 %custom-call.40 = f32[4,128,128]{2,1,0:T(8,128)S(1)} custom-call(f32[4,128,128]{2,1,0:T(8,128)S(1)} %convolution_subtract_fusion.3), custom_call_target="Cholesky" | custom-call | tf_op jit(solution)/shard_map/jit(cholesky)/cholesky | solution.py:34
  450.0 0.8 select_reduce_fusion.2
  451.1 6.7 broadcast_select_fusion
  457.8 15.3 %while.1 = (s32[]{:T(128)}, f32[4,512,512]{2,1,0:T(8,128)}, s32[4,2]{0,1:T(2,128)S(1)}, f32[4,4,128,128]{3,2,0,1:T(8,128)}, s32[]{:T(128)}) while((s32[]{:T(128)}, f32[4,512,512]{2,1,0:T(8,128)}, s32[4,2]{0,1:T(2,128)S(1)}, f32[4,4,128,128]{3,2,0,1:T(8,128)}, s32[]{:T(128)}) %tuple.40), condition=%wide.while_cond, body=%wide.while_body.sunk | while | flops 2 | bytes 525421 | solution.py:36
  457.9 0.6 fusion.71
  458.5 3.2 bitcast_dynamic-update-slice_fusion.2
  461.8 0.6 fusion.71
  462.4 3.2 bitcast_dynamic-update-slice_fusion.2
  465.6 0.6 fusion.71
  466.2 3.2 bitcast_dynamic-update-slice_fusion.2
  469.5 0.6 fusion.71
  470.1 3.1 bitcast_dynamic-update-slice_fusion.2
  473.1 158.2 %custom-call.41 = f32[4,4,128,128]{2,3,1,0:T(8,128)S(1)} custom-call(f32[4,4,128,128]{3,2,1,0:T(8,128)} %bitcast.104), custom_call_target="InvertDiagBlocksLowerTriangular" | custom-call | tf_op jit(solution)/shard_map/triangular_solve | solution.py:36
  631.3 1.0 fusion.35
  632.4 1.9 convolution_subtract_fusion
  634.3 1.1 fusion.40
  635.4 2.4 fusion.19
  637.9 2.0 fusion.38
  639.9 3.3 fusion.16
  643.2 3.1 fusion.37
  646.3 13.3 %multiply_bitcast_fusion = f32[4,1024,128]{1,2,0:T(8,128)} fusion(f32[4,1024,512]{2,1,0:T(8,128)} %all-gather.2.cloned.1.call-done, s32[]{:T(128)S(6)} %select_n.29, f32[4,128,512]{2,1,0:T(8,128)S(1)} %fusion.35, f32[4,128,512]{2,1,0:T(8,128)S(1)} %fusion.40, f32[4,128,512]{2,1,0:T(8,128)S(1)} %fusion.38, f32[4,128,512]{2,1,0:T(8,128)} %fusion.37, ...), kind=kOutput, calls=%fused_computation.28 | convolution fusion | flops 3222536192 | bytes 14696452 | tf_op jit(solution)/shard_map/srk,skc->src/dot_general | solution.py:39
  659.6 1.9 copy.98
  661.5 6.7 gather_fusion.1
  668.3 6.7 gather_fusion
  675.0 25.8 %fusion.2 = f32[4,36,128,128]{3,2,1,0:T(8,128)} fusion(f32[36,4,128,128]{3,2,1,0:T(8,128)} %gather_fusion.1, f32[36,4,128,128]{3,2,1,0:T(8,128)} %gather_fusion), kind=kOutput, calls=%fused_computation.8 | convolution fusion | flops 3623878656 | bytes 28311552 | tf_op jit(solution)/shard_map/spac,spbc->spab/dot_general | solution.py:50
  700.8 6.2 broadcast_in_dim.43
  706.9 26.3 %scatter_fusion = f32[192,128,128]{2,1,0:T(8,128)} fusion(f32[192,128,128]{2,1,0:T(8,128)} %broadcast_in_dim.43, s32[144]{0:T(256)S(1)} %bitcast.102, f32[144,128,128]{2,1,0:T(8,128)} %bitcast.98), kind=kCustom, calls=%fused_computation.3 | custom fusion | bytes 28312128 | tf_op jit(solution)/shard_map/scatter | solution.py:66
  733.3 10.5 all-to-all-start.2
  744.4 0.7 reduce.29
  745.2 273.1 %all-to-all-done.2 = f32[192,128,128]{2,1,0:T(8,128)} async-done(((f32[192,128,128]{2,1,0:T(8,128)}), f32[192,128,128]{2,1,0:T(8,128)}, u32[]{:S(2)}, u32[]{:S(2)}) %all-to-all-start.2) | async-done | bytes 12582944 | tf_op jit(solution)/shard_map/all_to_all | solution.py:68
  1018.4 15.5 %fusion = f32[8,128,128]{2,0,1:T(8,128)S(1)} fusion(f32[192,128,128]{2,1,0:T(8,128)} %all-to-all-done.2, s32[192]{0:T(256)S(1)} %eq.54), kind=kOutput, calls=%fused_computation.6 | convolution fusion | flops 301991424 | bytes 13107968 | tf_op jit(solution)/shard_map/ri,rab->iab/dot_general | solution.py:74
  1033.8 0.9 copy.97
  1034.7 2.3 constant_dynamic-slice_fusion.1
  1037.0 21.2 %reduce-scatter.2.cloned.1.call-done = f32[2,128,128]{2,1,0:T(8,128)} async-done(((f32[8,128,128]{2,1,0:T(8,128)}), f32[2,128,128]{2,1,0:T(8,128)}) %reduce-scatter.2.cloned.1.call-update) | async-done | bytes 131088 | tf_op jit(solution)/shard_map/reduce_scatter | solution.py:75
  1058.2 1.6 sub.14
  (52 shorter events, 2.2 us)
Async XLA Ops:
  7.2 639.2 %all-gather.2.cloned.1.call-start = ((), (), s32[]{:S(2)}) async-start(), calls=%async_computation.4 | async-start | bytes 10485760 | tf_op jit(solution)/shard_map/all_gather | solution.py:41
  12.0 5.1 copy-start.4
  12.0 8.1 copy-start.6
  12.0 8.1 copy-start.5
  12.0 8.4 copy-start.7
  12.0 84.2 %all-to-all-start = ((f32[4,4,512,128]{2,3,1,0:T(8,128)}), f32[4,4,512,128]{2,3,1,0:T(8,128)}, u32[]{:S(2)}, u32[]{:S(2)}) async-start(f32[4,4,512,128]{2,3,1,0:T(8,128)} %stack.2), calls=%async_computation | async-start | bytes 8388608 | tf_op jit(solution)/shard_map/all_to_all | solution.py:32
  96.2 637.1 %all-to-all-start.1 = ((s32[64,3,1]{1,2,0:T(1,128)}), s32[64,3,1]{1,2,0:T(1,128)S(1)}, u32[]{:S(2)}, u32[]{:S(2)}) async-start(s32[64,3,1]{1,2,0:T(1,128)} %bitcast.22), calls=%async_computation.1 | async-start | bytes 65536 | tf_op jit(solution)/shard_map/all_to_all | solution.py:69
  124.8 2.0 copy-start.1
  631.3 4.1 copy-start.2
  661.5 6.8 copy-start
  733.3 285.1 %all-to-all-start.2 = ((f32[192,128,128]{2,1,0:T(8,128)}), f32[192,128,128]{2,1,0:T(8,128)}, u32[]{:S(2)}, u32[]{:S(2)}) async-start(f32[192,128,128]{2,1,0:T(8,128)} %scatter_fusion), calls=%async_computation.2 | async-start | bytes 25165824 | tf_op jit(solution)/shard_map/all_to_all | solution.py:68
  743.8 314.4 %reduce-scatter.2.cloned.1.call-start = ((), (), s32[]{:S(2)}) async-start(), calls=%async_computation.5 | async-start | bytes 655360 | tf_op jit(solution)/shard_map/reduce_scatter | solution.py:75
  745.2 313.0 %copy-start.3 = (f32[2,128,128]{2,1,0:T(8,128)S(1)}, f32[2,128,128]{2,1,0:T(8,128)}, u32[]{:S(2)}) copy-start(f32[2,128,128]{2,1,0:T(8,128)} %param.15) | copy-start | bytes 393220
Sparse Core Ops, SparseCore 0:
  9.8 127.4 all-gather.1
  1034.9 23.2 reduce-scatter.1
